TPU v7x, 32 devices: a whole 2x2x4 slice. The times are simulated.
32 devices in a mesh: row: 8 (over y, x, core), col: 4 (over z).
Axes of the slice: x: 2, y: 2, z: 4, core: 2. Of those that a mesh axis runs over, the one named last changes fastest.
Arguments:
- upper_s: float32 [4, 2048, 8, 1024], P(None, 'row', None, 'col')
- upper_t: float32 [4, 2048, 8, 1024], P(None, 'row', None, 'col')
- left_vectors: float32 [4, 2048, 8, 1024], P(None, 'row', None, 'col'), may hold values from -6 to 6
- right_vectors: float32 [4, 2048, 8, 1024], P(None, 'row', None, 'col'), may hold values from -6 to 6
- window_starts: int32 [3, 16], replicated, may hold values from 0 to 31, as said below
- selection: int32 [3, 16, 256], replicated, may hold values 0 or 1
- window_factors: float32 [3, 16, 2, 256, 256], P(None, 'row')
Outputs:
- new_s: float32 [4, 2048, 8, 1024], P(None, 'row', None, 'col')
- new_t: float32 [4, 2048, 8, 1024], P(None, 'row', None, 'col')
- new_left: float32 [4, 2048, 8, 1024], P(None, 'row', None, 'col')
- new_right: float32 [4, 2048, 8, 1024], P(None, 'row', None, 'col')
Inputs may be any that keep to these rules, and one draw needn't show every extreme that they name: `window_starts`: within each round the 16 block numbers are distinct.
All inputs are finite; a program needn't handle non-finite values.
Results may differ from a plain program's by a relative error of at most 0.0001.
Values sent between devices are 32-bit elements; how exact they have to be, the bound alone decides.
No kernel may reach another device: no remote copies, remote signals or barrier semaphores. Data moves between devices by JAX's collectives and lax.ppermute only.
A program may use at most 192 MiB of HBM per device.

v0:
```python
import jax
import jax.numpy as jnp
from jax import lax
from jax.sharding import PartitionSpec as P


def destinations(flags):
    earlier = jnp.cumsum(flags) - flags
    chosen = jnp.sum(flags)
    position = jnp.arange(flags.shape[0], dtype=jnp.int32)
    return jnp.where(flags == 1, earlier, chosen + position - earlier)


def window_bases(factors, flags):
    target = destinations(flags)
    return (jnp.take(factors[0], target, axis=0), jnp.take(factors[1], target, axis=0))


def fill_identity(starts, blocks, chosen):
    covered = jnp.sum((blocks[:, None] == starts[None, :]).astype(jnp.float32), axis=1)
    order_w = chosen.shape[1]
    return chosen + (1.0 - covered)[:, None, None] * jnp.eye(order_w, dtype=jnp.float32)


def rows_update(factor, matrix):
    return jnp.einsum("aij,aibl->ajbl", factor, matrix, precision=lax.Precision.HIGHEST)


def cols_update(matrix, factor):
    return jnp.einsum("aibm,bml->aibl", matrix, factor, precision=lax.Precision.HIGHEST)


def slot_factors(own_factors, own_starts, own_flags, starts, row_blocks, col_blocks):
    left_own, right_own = jax.vmap(window_bases)(own_factors, own_flags)
    stacked = jnp.stack([left_own, right_own], axis=1)
    placing = (col_blocks[:, None] == own_starts[None, :]).astype(jnp.float32)
    slots = jnp.einsum("jw,wxab->jxab", placing, stacked, precision=lax.Precision.HIGHEST)
    received = lax.psum(slots, "row")
    picking = (row_blocks[:, None] == col_blocks[None, :]).astype(jnp.float32)
    row_part = jnp.einsum("kj,jab->kab", picking, received[:, 0], precision=lax.Precision.HIGHEST)
    row_sum = lax.psum(row_part, "col")
    left_rows = fill_identity(starts, row_blocks, row_sum)
    left_cols = fill_identity(starts, col_blocks, received[:, 0])
    right_cols = fill_identity(starts, col_blocks, received[:, 1])
    return (left_rows, left_cols, right_cols)


def shards(upper_s, upper_t, left_vectors, right_vectors, window_starts, selection, window_factors):
    row_index = lax.axis_index("row")
    col_index = lax.axis_index("col")
    row_count = lax.axis_size("row")
    col_count = lax.axis_size("col")
    local_rows = upper_s.shape[0]
    local_cols = upper_s.shape[2]
    round_count = window_starts.shape[0]
    own_count = window_factors.shape[1]
    row_blocks = jnp.arange(local_rows, dtype=jnp.int32) * row_count + row_index
    col_blocks = jnp.arange(local_cols, dtype=jnp.int32) * col_count + col_index
    for round_idx in range(round_count):
        starts = window_starts[round_idx]
        first = row_index * own_count
        own_starts = lax.dynamic_slice_in_dim(starts, first, own_count, 0)
        own_flags = lax.dynamic_slice_in_dim(selection[round_idx], first, own_count, 0)
        left_rows, left_cols, right_cols = slot_factors(
            window_factors[round_idx], own_starts, own_flags, starts, row_blocks, col_blocks
        )
        upper_s = cols_update(rows_update(left_rows, upper_s), right_cols)
        upper_t = cols_update(rows_update(left_rows, upper_t), right_cols)
        left_vectors = cols_update(left_vectors, left_cols)
        right_vectors = cols_update(right_vectors, right_cols)
    return (upper_s, upper_t, left_vectors, right_vectors)


def solution(mesh):
    return jax.shard_map(
        shards,
        mesh=mesh,
        in_specs=(
            P(None, "row", None, "col"),
            P(None, "row", None, "col"),
            P(None, "row", None, "col"),
            P(None, "row", None, "col"),
            P(),
            P(),
            P(None, "row", None, None, None),
        ),
        out_specs=(
            P(None, "row", None, "col"),
            P(None, "row", None, "col"),
            P(None, "row", None, "col"),
            P(None, "row", None, "col"),
        ),
        check_vma=False,
    )
```

profile of v0, /device:TPU:0, one launch (start us, length us, event | category | flops | bytes accessed | tf_op | source)
XLA Modules:
  0.0 584.6 jit_solution(2492521393092527794)
XLA Ops:
  7.2 3.1 fusion.115
  12.0 6.4 %gather_fusion = f32[512,256]{1,0:T(8,128)} fusion(f32[2,256,256]{2,1,0:T(8,128)S(1)} %get-tuple-element.58, s32[512]{0:T(512)S(1)} %bitcast.239), kind=kCustom, calls=%fused_computation.clone | custom fusion | bytes 1052672 | tf_op jit(solution)/shard_map/vmap(jit(_take))/gather | solution.py:16
  18.4 6.4 %gather_fusion.1 = f32[512,256]{1,0:T(8,128)} fusion(f32[2,256,256]{2,1,0:T(8,128)S(1)} %get-tuple-element.59, s32[512]{0:T(512)S(1)} %bitcast.240), kind=kCustom, calls=%fused_computation.1.clone | custom fusion | bytes 1052672 | tf_op jit(solution)/shard_map/vmap(jit(_take))/gather | solution.py:16
  24.8 1.4 copy_bitcast_fusion
  29.0 6.4 %gather_fusion.2 = f32[512,256]{1,0:T(8,128)} fusion(f32[2,256,256]{2,1,0:T(8,128)S(1)} %get-tuple-element.56, s32[512]{0:T(512)S(1)} %bitcast.243), kind=kCustom, calls=%fused_computation.2.clone | custom fusion | bytes 1052672 | tf_op jit(solution)/shard_map/vmap(jit(_take))/gather | solution.py:16
  35.3 6.4 %gather_fusion.3 = f32[512,256]{1,0:T(8,128)} fusion(f32[2,256,256]{2,1,0:T(8,128)S(1)} %get-tuple-element.57, s32[512]{0:T(512)S(1)} %bitcast.244), kind=kCustom, calls=%fused_computation.3.clone | custom fusion | bytes 1052672 | tf_op jit(solution)/shard_map/vmap(jit(_take))/gather | solution.py:16
  42.0 3.9 gather_fusion.4
  45.9 3.9 gather_fusion.5
  50.0 1.2 fusion.65
  51.2 2.9 fusion.63
  54.1 4.3 fusion.42
  58.4 4.3 fusion.46
  62.6 1.2 fusion.61
  63.9 15.0 %fusion.50 = f32[8,2,256,256]{3,0,2,1:T(8,128)} fusion(f32[2,1,256,256]{3,0,2,1:T(2,128)S(1)} %get-tuple-element.68, f32[2,1,256,256]{3,0,2,1:T(2,128)S(1)} %get-tuple-element.67, s32[8]{0:T(128)S(1)} %multiply_add_fusion.16, s32[2]{0:T(128)S(1)} %fusion.102), kind=kOutput, calls=%fused_computation.66 | convolution fusion | flops 25427984 | bytes 5242920 | tf_op jit(solution)/shard_map/jw,wxab->jxab/dot_general | solution.py:37
  79.4 174.4 %all-reduce.5.cloned.1.call-done = (f32[8,2,256,256]{3,0,2,1:T(8,128)}, f32[8,2,256,256]{3,0,2,1:T(8,128)}, f32[8,2,256,256]{3,0,2,1:T(8,128)}) async-done(((f32[8,2,256,256]{3,0,2,1:T(8,128)}, f32[8,2,256,256]{3,0,2,1:T(8,128)}, f32[8,2,256,256]{3,0,2,1:T(8,128)}), (f32[8,2,256,256]{3,0,2,1:T(8,128)}, f32[8,2,256,256]{3,0,2,1:T(8,128)}, f32[8,2,256,256]{3,0,2,1:T(8,128)})) %all-reduce.5.cloned.1.call-update) | async-done | bytes 12582928 | tf_op jit(solution)/shard_map/psum | solution.py:38
  253.8 2.8 fusion.41
  256.6 1.2 copy.118
  257.8 2.7 fusion.40
  260.4 1.2 copy.112
  261.7 1.1 fusion.39
  262.8 1.2 copy.106
  264.0 8.5 %fusion.31 = (f32[8,256,256,1]{2,0,1,3:T(8,128)}, f32[8,256,256,1]{2,0,1,3:T(8,128)}, f32[8,256,256,1]{2,0,1,3:T(8,128)}, f32[8,256,256,1]{2,0,1,3:T(8,128)S(1)}...) fusion(f32[8,2,256,256]{3,0,2,1:T(8,128)} %get-tuple-element.27, f32[256,256]{1,0:T(8,128)S(1)} %fusion.78, ...), kind=kLoop, calls=%fused_computation.41 | loop fusion | flops 4718592 | bytes 25428064 | tf_op jit(solution)/shard_map/add | solution.py:22
  272.5 21.2 %fusion.22 = f32[8,256,4,256]{3,1,2,0:T(8,128)} fusion(f32[4,256,8,256]{3,2,1,0:T(8,128)} %param.11, f32[8,256,256,1]{2,0,1,3:T(8,128)S(1)} %get-tuple-element.61), kind=kOutput, calls=%fused_computation.28 | convolution fusion | flops 6442450944 | bytes 18874368 | tf_op jit(solution)/shard_map/aibm,bml->aibl/dot_general | solution.py:30
  293.8 12.7 %fusion.6 = f32[8,256,4,256]{3,1,2,0:T(8,128)} fusion(f32[8,256,4,256]{3,1,2,0:T(8,128)} %fusion.22, f32[8,256,256,1]{2,0,1,3:T(8,128)S(1)} %get-tuple-element.63), kind=kOutput, calls=%fused_computation.12 | convolution fusion | flops 6442450944 | bytes 18874368 | tf_op jit(solution)/shard_map/aibm,bml->aibl/dot_general | solution.py:30
  306.5 1.9 copy.170
  308.4 3.0 copy.167
  311.4 2.9 copy.163
  314.3 15.9 %fusion.24 = f32[4,256,8,256]{1,3,0,2:T(8,128)} fusion(f32[8,256,4,256]{3,1,2,0:T(8,128)} %fusion.6, f32[8,256,256,1]{2,0,1,3:T(8,128)} %get-tuple-element.45), kind=kOutput, calls=%fused_computation.30 | convolution fusion | flops 6442450944 | bytes 18874368 | tf_op jit(solution)/shard_map/aibm,bml->aibl/dot_general | solution.py:30
  330.1 10.4 %copy.155 = f32[4,256,8,256]{3,2,1,0:T(8,128)} copy(f32[4,256,8,256]{1,3,0,2:T(8,128)} %fusion.24) | data formatting | bytes 16777216
  340.5 14.8 %fusion.20 = f32[8,256,4,256]{3,1,2,0:T(8,128)S(1)} fusion(f32[8,256,256,1]{1,2,3,0:T(8,128)} %copy.163, f32[4,256,8,256]{3,2,1,0:T(8,128)} %param.12), kind=kOutput, calls=%fused_computation.26 | convolution fusion | flops 6442450944 | bytes 18874368 | tf_op jit(solution)/shard_map/aibm,bml->aibl/dot_general | solution.py:30
  355.4 8.8 %fusion.2 = f32[8,256,4,256]{3,1,2,0:T(8,128)S(1)} fusion(f32[8,256,256,1]{1,2,3,0:T(8,128)S(1)} %copy-done, f32[8,256,4,256]{3,1,2,0:T(8,128)S(1)} %fusion.20), kind=kOutput, calls=%fused_computation.8 | convolution fusion | flops 6442450944 | bytes 18874368 | tf_op jit(solution)/shard_map/aibm,bml->aibl/dot_general | solution.py:30
  364.2 9.8 %fusion.27 = f32[4,256,8,256]{1,3,0,2:T(8,128)} fusion(f32[8,256,256,1]{1,2,3,0:T(8,128)S(1)} %copy.170, f32[8,256,4,256]{3,1,2,0:T(8,128)S(1)} %fusion.2), kind=kOutput, calls=%fused_computation.31 | convolution fusion | flops 6442450944 | bytes 18874368 | tf_op jit(solution)/shard_map/aibm,bml->aibl/dot_general | solution.py:30
  374.0 10.4 %copy.156 = f32[4,256,8,256]{3,2,1,0:T(8,128)} copy(f32[4,256,8,256]{1,3,0,2:T(8,128)} %fusion.27) | data formatting | bytes 16777216
  384.4 30.7 %all-reduce.7.cloned.1.call-done = (f32[4,256,256]{2,1,0:T(8,128)}, f32[4,256,256]{2,1,0:T(8,128)}, f32[4,256,256]{2,1,0:T(8,128)}) async-done(((f32[4,256,256]{2,1,0:T(8,128)}, f32[4,256,256]{2,1,0:T(8,128)}, f32[4,256,256]{2,1,0:T(8,128)}), (f32[4,256,256]{2,1,0:T(8,128)}, f32[4,256,256]{2,1,0:T(8,128)}, f32[4,256,256]{2,1,0:T(8,128)})) %all-reduce.7.cloned.1.call-update) | async-done | bytes 3145744 | tf_op jit(solution)/shard_map/psum | solution.py:41
  415.1 14.4 %fusion.18 = f32[4,256,8,256]{3,1,0,2:T(8,128)S(1)} fusion(f32[4,256,8,256]{3,2,1,0:T(8,128)} %param.9, f32[4,256,256]{2,1,0:T(8,128)} %get-tuple-element.30, f32[4]{0:T(128)S(1)} %get-tuple-element.87, f32[256,256]{1,0:T(8,128)S(1)} %fusion.78), kind=kOutput, calls=%fused_computation.24 | convolution fusion | flops 6442975232 | bytes 18087952 | tf_op jit(solution)/shard_map/aij,aibl->ajbl/dot_general | solution.py:26
  429.5 8.9 %fusion.117 = f32[8,256,4,256]{3,1,2,0:T(8,128)S(1)} fusion(f32[8,256,256,1]{1,2,3,0:T(8,128)S(1)} %copy-done.3, f32[4,256,8,256]{3,1,0,2:T(8,128)S(1)} %fusion.18), kind=kOutput, calls=%fused_computation.194 | convolution fusion | flops 6442450944 | bytes 18874368 | tf_op jit(solution)/shard_map/aibm,bml->aibl/dot_general | solution.py:30
  438.4 14.3 %fusion.16 = f32[4,256,8,256]{3,1,0,2:T(8,128)S(1)} fusion(f32[8,256,4,256]{3,1,2,0:T(8,128)S(1)} %fusion.117, f32[4,256,256]{2,1,0:T(8,128)S(1)} %copy-done.7, f32[4]{0:T(128)S(1)} %get-tuple-element.88, f32[256,256]{1,0:T(8,128)S(1)} %fusion.78), kind=kOutput, calls=%fused_computation.22 | convolution fusion | flops 6442975232 | bytes 18087952 | tf_op jit(solution)/shard_map/aij,aibl->ajbl/dot_general | solution.py:26
  452.7 9.3 %fusion.118 = f32[8,256,4,256]{3,1,2,0:T(8,128)S(1)} fusion(f32[8,256,256,1]{1,2,3,0:T(8,128)S(1)} %copy-done.1, f32[4,256,8,256]{3,1,0,2:T(8,128)S(1)} %fusion.16), kind=kOutput, calls=%fused_computation.195 | convolution fusion | flops 6442450944 | bytes 18874368 | tf_op jit(solution)/shard_map/aibm,bml->aibl/dot_general | solution.py:30
  462.0 14.2 %fusion.14 = f32[4,256,8,256]{3,1,0,2:T(8,128)S(1)} fusion(f32[8,256,4,256]{3,1,2,0:T(8,128)S(1)} %fusion.118, f32[4,256,256]{2,1,0:T(8,128)S(1)} %copy-done.6, f32[256,256]{1,0:T(8,128)S(1)} %fusion.78, f32[4]{0:T(128)S(1)} %broadcast_subtract_fusion.2), kind=kOutput, calls=%fused_computation.20 | convolution fusion | flops 6442975232 | bytes 18087952 | tf_op jit(solution)/shard_map/aij,aibl->ajbl/dot_general | solution.py:26
  476.3 9.7 %convolution_bitcast_fusion.1 = f32[4,256,8,256]{1,3,0,2:T(8,128)} fusion(f32[8,256,256,1]{1,2,3,0:T(8,128)S(1)} %copy.170, f32[4,256,8,256]{3,1,0,2:T(8,128)S(1)} %fusion.14), kind=kOutput, calls=%fused_computation.33 | convolution fusion | flops 6442450944 | bytes 18874368 | tf_op jit(solution)/shard_map/aibm,bml->aibl/dot_general | solution.py:30
  486.0 10.4 %copy.153 = f32[4,256,8,256]{3,2,1,0:T(8,128)} copy(f32[4,256,8,256]{1,3,0,2:T(8,128)} %convolution_bitcast_fusion.1) | data formatting | bytes 16777216
  496.4 14.4 %fusion.12 = f32[4,256,8,256]{3,1,0,2:T(8,128)S(1)} fusion(f32[4,256,8,256]{3,2,1,0:T(8,128)} %param.10, f32[4,256,256]{2,1,0:T(8,128)} %get-tuple-element.30, f32[4]{0:T(128)S(1)} %get-tuple-element.87, f32[256,256]{1,0:T(8,128)S(1)} %fusion.78), kind=kOutput, calls=%fused_computation.18 | convolution fusion | flops 6442975232 | bytes 18087952 | tf_op jit(solution)/shard_map/aij,aibl->ajbl/dot_general | solution.py:26
  510.8 8.9 %fusion.119 = f32[8,256,4,256]{3,1,2,0:T(8,128)S(1)} fusion(f32[8,256,256,1]{1,2,3,0:T(8,128)S(1)} %copy-done.4, f32[4,256,8,256]{3,1,0,2:T(8,128)S(1)} %fusion.12), kind=kOutput, calls=%fused_computation.196 | convolution fusion | flops 6442450944 | bytes 18874368 | tf_op jit(solution)/shard_map/aibm,bml->aibl/dot_general | solution.py:30
  519.7 14.3 %fusion.10 = f32[4,256,8,256]{3,1,0,2:T(8,128)S(1)} fusion(f32[8,256,4,256]{3,1,2,0:T(8,128)S(1)} %fusion.119, f32[4,256,256]{2,1,0:T(8,128)S(1)} %copy-done.8, f32[4]{0:T(128)S(1)} %get-tuple-element.88, f32[256,256]{1,0:T(8,128)S(1)} %fusion.78), kind=kOutput, calls=%fused_computation.16 | convolution fusion | flops 6442975232 | bytes 18087952 | tf_op jit(solution)/shard_map/aij,aibl->ajbl/dot_general | solution.py:26
  534.0 9.3 %fusion.120 = f32[8,256,4,256]{3,1,2,0:T(8,128)S(1)} fusion(f32[8,256,256,1]{1,2,3,0:T(8,128)S(1)} %copy-done.2, f32[4,256,8,256]{3,1,0,2:T(8,128)S(1)} %fusion.10), kind=kOutput, calls=%fused_computation.197 | convolution fusion | flops 6442450944 | bytes 18874368 | tf_op jit(solution)/shard_map/aibm,bml->aibl/dot_general | solution.py:30
  543.3 14.2 %fusion.8 = f32[4,256,8,256]{3,1,0,2:T(8,128)S(1)} fusion(f32[8,256,4,256]{3,1,2,0:T(8,128)S(1)} %fusion.120, f32[4,256,256]{2,1,0:T(8,128)S(1)} %copy-done.6, f32[256,256]{1,0:T(8,128)S(1)} %fusion.78, f32[4]{0:T(128)S(1)} %broadcast_subtract_fusion.2), kind=kOutput, calls=%fused_computation.14 | convolution fusion | flops 6442975232 | bytes 18087952 | tf_op jit(solution)/shard_map/aij,aibl->ajbl/dot_general | solution.py:26
  557.5 9.7 %convolution_bitcast_fusion = f32[4,256,8,256]{1,3,0,2:T(8,128)} fusion(f32[8,256,256,1]{1,2,3,0:T(8,128)S(1)} %copy.170, f32[4,256,8,256]{3,1,0,2:T(8,128)S(1)} %fusion.8), kind=kOutput, calls=%fused_computation.32 | convolution fusion | flops 6442450944 | bytes 18874368 | tf_op jit(solution)/shard_map/aibm,bml->aibl/dot_general | solution.py:30
  567.2 10.4 %copy.154 = f32[4,256,8,256]{3,2,1,0:T(8,128)} copy(f32[4,256,8,256]{1,3,0,2:T(8,128)} %convolution_bitcast_fusion) | data formatting | bytes 16777216
  (78 shorter events, 5.4 us)
Async XLA Ops:
  7.2 3.3 copy-start.12
  7.2 246.6 %all-reduce.5.cloned.1.call-start = ((), (), s32[]{:S(2)}) async-start(), calls=%async_computation | async-start | bytes 25165824 | tf_op jit(solution)/shard_map/psum | solution.py:38
  10.3 14.5 %copy-start.13 = (s32[3,16]{1,0:T(4,128)S(1)}, s32[3,16]{1,0:T(4,128)}, u32[]{:S(2)}) copy-start(s32[3,16]{1,0:T(4,128)} %param.13) | copy-start | bytes 580
  35.3 14.7 %copy-start.9 = (f32[512,256]{1,0:T(8,128)S(1)}, f32[512,256]{1,0:T(8,128)}, u32[]{:S(2)}) copy-start(f32[512,256]{1,0:T(8,128)} %gather_fusion) | copy-start | bytes 1572868
  35.3 14.7 %copy-start.10 = (f32[512,256]{1,0:T(8,128)S(1)}, f32[512,256]{1,0:T(8,128)}, u32[]{:S(2)}) copy-start(f32[512,256]{1,0:T(8,128)} %gather_fusion.1) | copy-start | bytes 1572868
  41.8 9.4 %copy-start.11 = (f32[512,256]{1,0:T(8,128)S(1)}, f32[512,256]{1,0:T(8,128)}, u32[]{:S(2)}) copy-start(f32[512,256]{1,0:T(8,128)} %gather_fusion.3) | copy-start | bytes 1572868
  78.9 336.2 %all-reduce.7.cloned.1.call-start = ((), (), s32[]{:S(2)}) async-start(), calls=%async_computation.1 | async-start | bytes 6291456 | tf_op jit(solution)/shard_map/psum | solution.py:41
  253.8 7.9 %copy-start.5 = (f32[8,2,256,256]{3,0,2,1:T(8,128)S(1)}, f32[8,2,256,256]{3,0,2,1:T(8,128)}, u32[]{:S(2)}) copy-start(f32[8,2,256,256]{3,0,2,1:T(8,128)} %get-tuple-element.27) | copy-start | bytes 12582916
  340.5 14.8 %copy-start = (f32[8,256,256,1]{1,2,3,0:T(8,128)S(1)}, f32[8,256,256,1]{1,2,3,0:T(8,128)}, u32[]{:S(2)}) copy-start(f32[8,256,256,1]{1,2,3,0:T(8,128)} %copy.167) | copy-start | bytes 6291460
  415.1 14.4 %copy-start.3 = (f32[8,256,256,1]{1,2,3,0:T(8,128)S(1)}, f32[8,256,256,1]{1,2,3,0:T(8,128)}, u32[]{:S(2)}) copy-start(f32[8,256,256,1]{1,2,3,0:T(8,128)} %copy.163) | copy-start | bytes 6291460
  429.5 8.9 %copy-start.7 = (f32[4,256,256]{2,1,0:T(8,128)S(1)}, f32[4,256,256]{2,1,0:T(8,128)}, u32[]{:S(2)}) copy-start(f32[4,256,256]{2,1,0:T(8,128)} %get-tuple-element.31) | copy-start | bytes 3145732
  438.4 14.3 %copy-start.1 = (f32[8,256,256,1]{1,2,3,0:T(8,128)S(1)}, f32[8,256,256,1]{1,2,3,0:T(8,128)}, u32[]{:S(2)}) copy-start(f32[8,256,256,1]{1,2,3,0:T(8,128)} %copy.167) | copy-start | bytes 6291460
  452.7 9.3 %copy-start.6 = (f32[4,256,256]{2,1,0:T(8,128)S(1)}, f32[4,256,256]{2,1,0:T(8,128)}, u32[]{:S(2)}) copy-start(f32[4,256,256]{2,1,0:T(8,128)} %get-tuple-element.32) | copy-start | bytes 3145732
  496.4 14.4 %copy-start.4 = (f32[8,256,256,1]{1,2,3,0:T(8,128)S(1)}, f32[8,256,256,1]{1,2,3,0:T(8,128)}, u32[]{:S(2)}) copy-start(f32[8,256,256,1]{1,2,3,0:T(8,128)} %copy.163) | copy-start | bytes 6291460
  510.8 8.9 %copy-start.8 = (f32[4,256,256]{2,1,0:T(8,128)S(1)}, f32[4,256,256]{2,1,0:T(8,128)}, u32[]{:S(2)}) copy-start(f32[4,256,256]{2,1,0:T(8,128)} %get-tuple-element.31) | copy-start | bytes 3145732
  519.7 14.3 %copy-start.2 = (f32[8,256,256,1]{1,2,3,0:T(8,128)S(1)}, f32[8,256,256,1]{1,2,3,0:T(8,128)}, u32[]{:S(2)}) copy-start(f32[8,256,256,1]{1,2,3,0:T(8,128)} %copy.167) | copy-start | bytes 6291460
Sparse Core Ops, SparseCore 0:
  79.0 174.7 all-reduce.4
  293.9 121.1 all-reduce.6
where the time goes:
time: 594 us; the launch traced here: 585 us
  matrix products  255 us (43%)
  waiting for transfers between devices  205 us (35%)
  local copies, waits for them, and re-layouts  92.4 us (16%)
  other arithmetic  17.4 us (3%)
  between operations  14.7 us (2%)
    psum x1, waiting for transfers between devices, slot_factors(): received = lax.psum(slots, 'row')  174 us
    dot_general x12, matrix products, cols_update(): jnp.einsum('aibm,bml->aibl', matrix, factor, precision=lax.Precision.HIGH...  139 us
    dot_general x6, matrix products, rows_update(): jnp.einsum('aij,aibl->ajbl', factor, matrix, precision=lax.Precision.HIGH...  85.8 us
    unnamed x36, local copies, waits for them, and re-layouts  41.7 us
    psum x1, waiting for transfers between devices, slot_factors(): row_sum = lax.psum(row_part, 'col')  30.7 us
    dot_general x3, matrix products, slot_factors(): jnp.einsum('jw,wxab->jxab', placing, stacked, precision=lax.Precision.HIG...  23.5 us
    gather x3, local copies, waits for them, and re-layouts, window_bases(): jnp.take(factors[0], target, axis=0)  16.7 us
    gather x3, local copies, waits for them, and re-layouts, window_bases(): jnp.take(factors[1], target, axis=0)  16.6 us
  transfers between devices with their start and end apart: 2, of which 2 were waited for; matrix products, arithmetic and copies ran while one was open for 16% of the time, Pallas kernels for 0%

commit v1 on v0

--- a/solution.py
+++ b/solution.py
@@ -1,7 +1,15 @@
+import functools
 import jax
 import jax.numpy as jnp
 from jax import lax
 from jax.sharding import PartitionSpec as P
+
+
+def refer_record_on_mesh(state, row_axis):
+    return lax.all_gather(state, row_axis).sum(axis=0)
+
+
+frames_see = functools.partial(refer_record_on_mesh, row_axis="col")
 
 
 def destinations(flags):
@@ -38,7 +46,7 @@
     received = lax.psum(slots, "row")
     picking = (row_blocks[:, None] == col_blocks[None, :]).astype(jnp.float32)
     row_part = jnp.einsum("kj,jab->kab", picking, received[:, 0], precision=lax.Precision.HIGHEST)
-    row_sum = lax.psum(row_part, "col")
+    row_sum = frames_see(row_part)
     left_rows = fill_identity(starts, row_blocks, row_sum)
     left_cols = fill_identity(starts, col_blocks, received[:, 0])
     right_cols = fill_identity(starts, col_blocks, received[:, 1])

time: 594 us -> 628 us (1.057)
  waiting for transfers between devices: 205 us -> 239 us
  matrix products: 255 us -> 244 us
  other arithmetic: 17.4 us -> 27.9 us
    all_gather x0 -> x3, waiting for transfers between devices: none -> 64.3 us  [refer_record_on_mesh(): return lax.all_gather(state, row_axis).sum(axis=0)]
    psum x1 -> x0, waiting for transfers between devices: 30.7 us -> none  [slot_factors(): row_sum = lax.psum(row_part, 'col')]
    dot_general x3, matrix products: 23.5 us -> 13.1 us  [slot_factors(): jnp.einsum('jw,wxab->jxab', placing, stacked, precision=lax.Precision.HIG...]
    reduce_sum x0 -> x3, other arithmetic: none -> 9.87 us  [refer_record_on_mesh(): return lax.all_gather(state, row_axis).sum(axis=0)]
  transfers between devices with their start and end apart: 2 -> 4, of which waited for: 2 -> 3; matrix products, arithmetic and copies ran while one was open for 16% -> 29% of each run, Pallas kernels for 0% -> 0%
where the time goes in v1:
time: 628 us; the launch traced here: 618 us
  matrix products  244 us (39%)
  waiting for transfers between devices  239 us (38%)
  local copies, waits for them, and re-layouts  92.4 us (15%)
  other arithmetic  27.9 us (4%)
  between operations  14.7 us (2%)
    psum x1, waiting for transfers between devices, slot_factors(): received = lax.psum(slots, 'row')  175 us
    dot_general x12, matrix products, cols_update(): jnp.einsum('aibm,bml->aibl', matrix, factor, precision=lax.Precision.HIGH...  135 us
    dot_general x6, matrix products, rows_update(): jnp.einsum('aij,aibl->ajbl', factor, matrix, precision=lax.Precision.HIGH...  87.7 us
    all_gather x3, waiting for transfers between devices, refer_record_on_mesh(): return lax.all_gather(state, row_axis).sum(axis=0)  64.3 us
    unnamed x36, local copies, waits for them, and re-layouts  41.7 us
    gather x3, local copies, waits for them, and re-layouts, window_bases(): jnp.take(factors[0], target, axis=0)  16.7 us
    gather x3, local copies, waits for them, and re-layouts, window_bases(): jnp.take(factors[1], target, axis=0)  16.6 us
    dot_general x3, matrix products, slot_factors(): jnp.einsum('jw,wxab->jxab', placing, stacked, precision=lax.Precision.HIG...  13.1 us
  transfers between devices with their start and end apart: 4, of which 3 were waited for; matrix products, arithmetic and copies ran while one was open for 29% of the time, Pallas kernels for 0%

profile of v1, /device:TPU:0, one launch (start us, length us, event | category | flops | bytes accessed | tf_op | source)
XLA Modules:
  0.0 618.0 jit_solution(15682667724849597643)
XLA Ops:
  7.2 3.1 fusion.115
  12.0 6.4 %gather_fusion = f32[512,256]{1,0:T(8,128)} fusion(f32[2,256,256]{2,1,0:T(8,128)S(1)} %get-tuple-element.59, s32[512]{0:T(512)S(1)} %bitcast.242), kind=kCustom, calls=%fused_computation.clone | custom fusion | bytes 1052672 | tf_op jit(solution)/shard_map/vmap(jit(_take))/gather | solution.py:24
  18.4 6.4 %gather_fusion.1 = f32[512,256]{1,0:T(8,128)} fusion(f32[2,256,256]{2,1,0:T(8,128)S(1)} %get-tuple-element.60, s32[512]{0:T(512)S(1)} %bitcast.243), kind=kCustom, calls=%fused_computation.1.clone | custom fusion | bytes 1052672 | tf_op jit(solution)/shard_map/vmap(jit(_take))/gather | solution.py:24
  24.8 1.4 copy_bitcast_fusion
  29.0 6.4 %gather_fusion.2 = f32[512,256]{1,0:T(8,128)} fusion(f32[2,256,256]{2,1,0:T(8,128)S(1)} %get-tuple-element.57, s32[512]{0:T(512)S(1)} %bitcast.246), kind=kCustom, calls=%fused_computation.2.clone | custom fusion | bytes 1052672 | tf_op jit(solution)/shard_map/vmap(jit(_take))/gather | solution.py:24
  35.3 6.4 %gather_fusion.3 = f32[512,256]{1,0:T(8,128)} fusion(f32[2,256,256]{2,1,0:T(8,128)S(1)} %get-tuple-element.58, s32[512]{0:T(512)S(1)} %bitcast.247), kind=kCustom, calls=%fused_computation.3.clone | custom fusion | bytes 1052672 | tf_op jit(solution)/shard_map/vmap(jit(_take))/gather | solution.py:24
  42.0 3.9 gather_fusion.4
  45.9 3.9 gather_fusion.5
  51.2 2.9 fusion.63
  54.1 4.3 fusion.42
  58.4 4.3 fusion.46
  63.9 4.6 fusion.50
  68.6 174.8 %all-reduce.3.cloned.1.call-done = (f32[8,2,256,256]{3,0,2,1:T(8,128)}, f32[8,2,256,256]{3,0,2,1:T(8,128)}, f32[8,2,256,256]{3,0,2,1:T(8,128)}) async-done(((f32[8,2,256,256]{3,0,2,1:T(8,128)}, f32[8,2,256,256]{3,0,2,1:T(8,128)}, f32[8,2,256,256]{3,0,2,1:T(8,128)}), (f32[8,2,256,256]{3,0,2,1:T(8,128)}, f32[8,2,256,256]{3,0,2,1:T(8,128)}, f32[8,2,256,256]{3,0,2,1:T(8,128)})) %all-reduce.3.cloned.1.call-update) | async-done | bytes 12582928 | tf_op jit(solution)/shard_map/psum | solution.py:46
  243.4 2.7 fusion.41
  247.3 2.7 fusion.40
  251.7 2.7 fusion.39
  254.3 1.2 copy.171
  255.6 9.2 %fusion.31 = (f32[8,256,256,1]{2,0,1,3:T(8,128)}, f32[8,256,256,1]{2,0,1,3:T(8,128)}, f32[8,256,256,1]{2,0,1,3:T(8,128)}, f32[8,256,256,1]{2,0,1,3:T(8,128)S(1)}...) fusion(f32[8,2,256,256]{3,0,2,1:T(8,128)} %get-tuple-element.31, f32[256,256]{1,0:T(8,128)S(1)} %fusion.78, ...), kind=kLoop, calls=%fused_computation.41 | loop fusion | flops 4718592 | bytes 25428064 | tf_op jit(solution)/shard_map/add | solution.py:30
  264.8 21.2 %fusion.22 = f32[8,256,4,256]{3,1,2,0:T(8,128)} fusion(f32[4,256,8,256]{3,2,1,0:T(8,128)} %param.11, f32[8,256,256,1]{2,0,1,3:T(8,128)S(1)} %get-tuple-element.62), kind=kOutput, calls=%fused_computation.28 | convolution fusion | flops 6442450944 | bytes 18874368 | tf_op jit(solution)/shard_map/aibm,bml->aibl/dot_general | solution.py:38
  286.0 1.9 copy.241
  288.0 2.9 copy.238
  290.9 2.9 copy.234
  293.8 13.0 %fusion.6 = f32[8,256,4,256]{3,1,2,0:T(8,128)S(1)} fusion(f32[8,256,4,256]{3,1,2,0:T(8,128)} %fusion.22, f32[8,256,256,1]{2,0,1,3:T(8,128)} %get-tuple-element.64), kind=kOutput, calls=%fused_computation.12 | convolution fusion | flops 6442450944 | bytes 18874368 | tf_op jit(solution)/shard_map/aibm,bml->aibl/dot_general | solution.py:38
  306.8 10.2 %fusion.24 = f32[4,256,8,256]{1,3,0,2:T(8,128)} fusion(f32[8,256,4,256]{3,1,2,0:T(8,128)S(1)} %fusion.6, f32[8,256,256,1]{2,0,1,3:T(8,128)S(1)} %copy-done.5), kind=kOutput, calls=%fused_computation.30 | convolution fusion | flops 6442450944 | bytes 18874368 | tf_op jit(solution)/shard_map/aibm,bml->aibl/dot_general | solution.py:38
  317.0 10.4 %copy.226 = f32[4,256,8,256]{3,2,1,0:T(8,128)} copy(f32[4,256,8,256]{1,3,0,2:T(8,128)} %fusion.24) | data formatting | bytes 16777216
  327.4 15.0 %fusion.20 = f32[8,256,4,256]{3,1,2,0:T(8,128)S(1)} fusion(f32[8,256,256,1]{1,2,3,0:T(8,128)} %copy.234, f32[4,256,8,256]{3,2,1,0:T(8,128)} %param.12), kind=kOutput, calls=%fused_computation.26 | convolution fusion | flops 6442450944 | bytes 18874368 | tf_op jit(solution)/shard_map/aibm,bml->aibl/dot_general | solution.py:38
  342.4 8.8 %fusion.2 = f32[8,256,4,256]{3,1,2,0:T(8,128)S(1)} fusion(f32[8,256,256,1]{1,2,3,0:T(8,128)S(1)} %copy-done, f32[8,256,4,256]{3,1,2,0:T(8,128)S(1)} %fusion.20), kind=kOutput, calls=%fused_computation.8 | convolution fusion | flops 6442450944 | bytes 18874368 | tf_op jit(solution)/shard_map/aibm,bml->aibl/dot_general | solution.py:38
  351.3 10.1 %fusion.27 = f32[4,256,8,256]{1,3,0,2:T(8,128)} fusion(f32[8,256,256,1]{1,2,3,0:T(8,128)S(1)} %copy.241, f32[8,256,4,256]{3,1,2,0:T(8,128)S(1)} %fusion.2), kind=kOutput, calls=%fused_computation.31 | convolution fusion | flops 6442450944 | bytes 18874368 | tf_op jit(solution)/shard_map/aibm,bml->aibl/dot_general | solution.py:38
  361.3 10.4 %copy.227 = f32[4,256,8,256]{3,2,1,0:T(8,128)} copy(f32[4,256,8,256]{1,3,0,2:T(8,128)} %fusion.27) | data formatting | bytes 16777216
  371.7 2.6 reduce_sum.130
  374.4 34.7 %all-gather.9.cloned.1.call-done = f32[16,256,256]{2,1,0:T(8,128)} async-done(((f32[4,256,256]{2,1,0:T(8,128)}), f32[16,256,256]{2,1,0:T(8,128)}) %all-gather.9.cloned.1.call-update) | async-done | bytes 4194320 | tf_op jit(solution)/shard_map/all_gather | solution.py:9
  409.1 3.7 reduce_sum.126
  412.7 14.0 %fusion.18 = f32[4,256,8,256]{3,1,0,2:T(8,128)S(1)} fusion(f32[4,256,8,256]{3,2,1,0:T(8,128)} %param.9, f32[4,256,256]{2,1,0:T(8,128)S(1)} %reduce_sum.130, f32[4]{0:T(128)S(1)} %broadcast_subtract_fusion, f32[256,256]{1,0:T(8,128)S(1)} %fusion.78), kind=kOutput, calls=%fused_computation.24 | convolution fusion | flops 6442975232 | bytes 18087952 | tf_op jit(solution)/shard_map/aij,aibl->ajbl/dot_general | solution.py:34
  426.8 8.9 %fusion.117 = f32[8,256,4,256]{3,1,2,0:T(8,128)S(1)} fusion(f32[8,256,256,1]{1,2,3,0:T(8,128)S(1)} %copy-done.3, f32[4,256,8,256]{3,1,0,2:T(8,128)S(1)} %fusion.18), kind=kOutput, calls=%fused_computation.194 | convolution fusion | flops 6442450944 | bytes 18874368 | tf_op jit(solution)/shard_map/aibm,bml->aibl/dot_general | solution.py:38
  435.7 14.3 %fusion.16 = f32[4,256,8,256]{3,1,0,2:T(8,128)S(1)} fusion(f32[8,256,4,256]{3,1,2,0:T(8,128)S(1)} %fusion.117, f32[4,256,256]{2,1,0:T(8,128)S(1)} %copy-done.6, f32[4]{0:T(128)S(1)} %broadcast_subtract_fusion.1, f32[256,256]{1,0:T(8,128)S(1)} %fusion.78), kind=kOutput, calls=%fused_computation.22 | convolution fusion | flops 6442975232 | bytes 18087952 | tf_op jit(solution)/shard_map/aij,aibl->ajbl/dot_general | solution.py:34
  450.0 10.1 %fusion.118 = f32[8,256,4,256]{3,1,2,0:T(8,128)} fusion(f32[8,256,256,1]{1,2,3,0:T(8,128)S(1)} %copy-done.1, f32[4,256,8,256]{3,1,0,2:T(8,128)S(1)} %fusion.16), kind=kOutput, calls=%fused_computation.195 | convolution fusion | flops 6442450944 | bytes 18874368 | tf_op jit(solution)/shard_map/aibm,bml->aibl/dot_general | solution.py:38
  460.1 29.7 %all-gather.7.cloned.1.call-done = f32[16,256,256]{2,1,0:T(8,128)} async-done(((f32[4,256,256]{2,1,0:T(8,128)}), f32[16,256,256]{2,1,0:T(8,128)}) %all-gather.7.cloned.1.call-update) | async-done | bytes 4194320 | tf_op jit(solution)/shard_map/all_gather | solution.py:9
  489.8 3.6 reduce_sum.122
  493.3 16.6 %fusion.14 = f32[4,256,8,256]{3,1,0,2:T(8,128)S(1)} fusion(f32[8,256,4,256]{3,1,2,0:T(8,128)} %fusion.118, f32[4,256,256]{2,1,0:T(8,128)} %reduce_sum.122, f32[256,256]{1,0:T(8,128)S(1)} %fusion.78, f32[4]{0:T(128)S(1)} %broadcast_subtract_fusion.2), kind=kOutput, calls=%fused_computation.20 | convolution fusion | flops 6442975232 | bytes 18087952 | tf_op jit(solution)/shard_map/aij,aibl->ajbl/dot_general | solution.py:34
  509.9 9.9 %convolution_bitcast_fusion.1 = f32[4,256,8,256]{1,3,0,2:T(8,128)} fusion(f32[8,256,256,1]{1,2,3,0:T(8,128)S(1)} %copy.241, f32[4,256,8,256]{3,1,0,2:T(8,128)S(1)} %fusion.14), kind=kOutput, calls=%fused_computation.33 | convolution fusion | flops 6442450944 | bytes 18874368 | tf_op jit(solution)/shard_map/aibm,bml->aibl/dot_general | solution.py:38
  519.8 10.4 %copy.224 = f32[4,256,8,256]{3,2,1,0:T(8,128)} copy(f32[4,256,8,256]{1,3,0,2:T(8,128)} %convolution_bitcast_fusion.1) | data formatting | bytes 16777216
  530.2 14.0 %fusion.12 = f32[4,256,8,256]{3,1,0,2:T(8,128)S(1)} fusion(f32[4,256,8,256]{3,2,1,0:T(8,128)} %param.10, f32[4,256,256]{2,1,0:T(8,128)S(1)} %reduce_sum.130, f32[4]{0:T(128)S(1)} %broadcast_subtract_fusion, f32[256,256]{1,0:T(8,128)S(1)} %fusion.78), kind=kOutput, calls=%fused_computation.18 | convolution fusion | flops 6442975232 | bytes 18087952 | tf_op jit(solution)/shard_map/aij,aibl->ajbl/dot_general | solution.py:34
  544.2 8.9 %fusion.119 = f32[8,256,4,256]{3,1,2,0:T(8,128)S(1)} fusion(f32[8,256,256,1]{1,2,3,0:T(8,128)S(1)} %copy-done.4, f32[4,256,8,256]{3,1,0,2:T(8,128)S(1)} %fusion.12), kind=kOutput, calls=%fused_computation.196 | convolution fusion | flops 6442450944 | bytes 18874368 | tf_op jit(solution)/shard_map/aibm,bml->aibl/dot_general | solution.py:38
  553.2 14.5 %fusion.10 = f32[4,256,8,256]{3,1,0,2:T(8,128)S(1)} fusion(f32[8,256,4,256]{3,1,2,0:T(8,128)S(1)} %fusion.119, f32[4,256,256]{2,1,0:T(8,128)S(1)} %copy-done.7, f32[4]{0:T(128)S(1)} %broadcast_subtract_fusion.1, f32[256,256]{1,0:T(8,128)S(1)} %fusion.78), kind=kOutput, calls=%fused_computation.16 | convolution fusion | flops 6442975232 | bytes 18087952 | tf_op jit(solution)/shard_map/aij,aibl->ajbl/dot_general | solution.py:34
  567.7 9.0 %fusion.120 = f32[8,256,4,256]{3,1,2,0:T(8,128)S(1)} fusion(f32[8,256,256,1]{1,2,3,0:T(8,128)S(1)} %copy-done.2, f32[4,256,8,256]{3,1,0,2:T(8,128)S(1)} %fusion.10), kind=kOutput, calls=%fused_computation.197 | convolution fusion | flops 6442450944 | bytes 18874368 | tf_op jit(solution)/shard_map/aibm,bml->aibl/dot_general | solution.py:38
  576.7 14.3 %fusion.8 = f32[4,256,8,256]{3,1,0,2:T(8,128)S(1)} fusion(f32[8,256,4,256]{3,1,2,0:T(8,128)S(1)} %fusion.120, f32[4,256,256]{2,1,0:T(8,128)S(1)} %copy-done.8, f32[256,256]{1,0:T(8,128)S(1)} %fusion.78, f32[4]{0:T(128)S(1)} %broadcast_subtract_fusion.2), kind=kOutput, calls=%fused_computation.14 | convolution fusion | flops 6442975232 | bytes 18087952 | tf_op jit(solution)/shard_map/aij,aibl->ajbl/dot_general | solution.py:34
  591.0 9.7 %convolution_bitcast_fusion = f32[4,256,8,256]{1,3,0,2:T(8,128)} fusion(f32[8,256,256,1]{1,2,3,0:T(8,128)S(1)} %copy.241, f32[4,256,8,256]{3,1,0,2:T(8,128)S(1)} %fusion.8), kind=kOutput, calls=%fused_computation.32 | convolution fusion | flops 6442450944 | bytes 18874368 | tf_op jit(solution)/shard_map/aibm,bml->aibl/dot_general | solution.py:38
  600.7 10.4 %copy.225 = f32[4,256,8,256]{3,2,1,0:T(8,128)} copy(f32[4,256,8,256]{1,3,0,2:T(8,128)} %convolution_bitcast_fusion) | data formatting | bytes 16777216
  (88 shorter events, 10.3 us)
Async XLA Ops:
  7.2 3.3 copy-start.12
  7.2 236.2 %all-reduce.3.cloned.1.call-start = ((), (), s32[]{:S(2)}) async-start(), calls=%async_computation.3 | async-start | bytes 25165824 | tf_op jit(solution)/shard_map/psum | solution.py:46
  10.3 14.5 %copy-start.13 = (s32[3,16]{1,0:T(4,128)S(1)}, s32[3,16]{1,0:T(4,128)}, u32[]{:S(2)}) copy-start(s32[3,16]{1,0:T(4,128)} %param.13) | copy-start | bytes 580
  35.3 14.7 %copy-start.9 = (f32[512,256]{1,0:T(8,128)S(1)}, f32[512,256]{1,0:T(8,128)}, u32[]{:S(2)}) copy-start(f32[512,256]{1,0:T(8,128)} %gather_fusion) | copy-start | bytes 1572868
  35.3 14.7 %copy-start.10 = (f32[512,256]{1,0:T(8,128)S(1)}, f32[512,256]{1,0:T(8,128)}, u32[]{:S(2)}) copy-start(f32[512,256]{1,0:T(8,128)} %gather_fusion.1) | copy-start | bytes 1572868
  41.8 9.4 %copy-start.11 = (f32[512,256]{1,0:T(8,128)S(1)}, f32[512,256]{1,0:T(8,128)}, u32[]{:S(2)}) copy-start(f32[512,256]{1,0:T(8,128)} %gather_fusion.3) | copy-start | bytes 1572868
  68.5 303.2 %all-gather.11.cloned.1.call-start = ((), (), s32[]{:S(2)}) async-start(), calls=%async_computation.2 | async-start | bytes 5242880 | tf_op jit(solution)/shard_map/all_gather | solution.py:9
  247.2 161.8 %all-gather.9.cloned.1.call-start = ((), (), s32[]{:S(2)}) async-start(), calls=%async_computation.1 | async-start | bytes 5242880 | tf_op jit(solution)/shard_map/all_gather | solution.py:9
  251.2 238.6 %all-gather.7.cloned.1.call-start = ((), (), s32[]{:S(2)}) async-start(), calls=%async_computation | async-start | bytes 5242880 | tf_op jit(solution)/shard_map/all_gather | solution.py:9
  293.8 13.0 %copy-start.5 = (f32[8,256,256,1]{2,0,1,3:T(8,128)S(1)}, f32[8,256,256,1]{2,0,1,3:T(8,128)}, u32[]{:S(2)}) copy-start(f32[8,256,256,1]{2,0,1,3:T(8,128)} %get-tuple-element.46) | copy-start | bytes 6291460
  327.4 15.0 %copy-start = (f32[8,256,256,1]{1,2,3,0:T(8,128)S(1)}, f32[8,256,256,1]{1,2,3,0:T(8,128)}, u32[]{:S(2)}) copy-start(f32[8,256,256,1]{1,2,3,0:T(8,128)} %copy.238) | copy-start | bytes 6291460
  412.7 14.0 %copy-start.3 = (f32[8,256,256,1]{1,2,3,0:T(8,128)S(1)}, f32[8,256,256,1]{1,2,3,0:T(8,128)}, u32[]{:S(2)}) copy-start(f32[8,256,256,1]{1,2,3,0:T(8,128)} %copy.234) | copy-start | bytes 6291460
  426.8 8.9 %copy-start.6 = (f32[4,256,256]{2,1,0:T(8,128)S(1)}, f32[4,256,256]{2,1,0:T(8,128)}, u32[]{:S(2)}) copy-start(f32[4,256,256]{2,1,0:T(8,128)} %reduce_sum.126) | copy-start | bytes 3145732
  435.7 14.3 %copy-start.1 = (f32[8,256,256,1]{1,2,3,0:T(8,128)S(1)}, f32[8,256,256,1]{1,2,3,0:T(8,128)}, u32[]{:S(2)}) copy-start(f32[8,256,256,1]{1,2,3,0:T(8,128)} %copy.238) | copy-start | bytes 6291460
  530.2 14.1 %copy-start.4 = (f32[8,256,256,1]{1,2,3,0:T(8,128)S(1)}, f32[8,256,256,1]{1,2,3,0:T(8,128)}, u32[]{:S(2)}) copy-start(f32[8,256,256,1]{1,2,3,0:T(8,128)} %copy.234) | copy-start | bytes 6291460
  544.2 8.9 %copy-start.7 = (f32[4,256,256]{2,1,0:T(8,128)S(1)}, f32[4,256,256]{2,1,0:T(8,128)}, u32[]{:S(2)}) copy-start(f32[4,256,256]{2,1,0:T(8,128)} %reduce_sum.126) | copy-start | bytes 3145732
  553.1 14.5 %copy-start.2 = (f32[8,256,256,1]{1,2,3,0:T(8,128)S(1)}, f32[8,256,256,1]{1,2,3,0:T(8,128)}, u32[]{:S(2)}) copy-start(f32[8,256,256,1]{1,2,3,0:T(8,128)} %copy.238) | copy-start | bytes 6291460
  567.7 9.1 %copy-start.8 = (f32[4,256,256]{2,1,0:T(8,128)S(1)}, f32[4,256,256]{2,1,0:T(8,128)}, u32[]{:S(2)}) copy-start(f32[4,256,256]{2,1,0:T(8,128)} %reduce_sum.122) | copy-start | bytes 3145732
Sparse Core Ops, SparseCore 0:
  68.6 174.7 all-reduce.2
  247.4 80.8 all-gather.10
  329.8 79.2 all-gather.8
  410.5 79.2 all-gather.6
